TPU v7x, 32 devices: a whole 2x2x4 slice. The times are simulated.
32 devices in a mesh: dp: 8 (over z, y), tensor: 4 (over x, core).
Axes of the slice: x: 2, y: 2, z: 4, core: 2. Of those that a mesh axis runs over, the one named last changes fastest.
Arguments:
- tokens: bfloat16 [8192, 1024], P(('dp', 'tensor')), may hold values from -6 to 6
- cotangent: float32 [8192, 1024], P(('dp', 'tensor')), may hold values from -6 to 6
- lengths: int32 [8, 2], P('dp'), may hold values from 64 to 512, as said below
- order: int32 [8, 1024], P('dp'), may hold values from 0 to 1023, each once within a row
- adapter_ids: int32 [8, 2], P('dp'), may hold values from 0 to 7
- norm1_gain: float32 [1024], replicated, may hold values from 0.25 to 1.75
- norm1_shift: float32 [1024], replicated, may hold values from -1.5 to 1.5
- qkv_weight: bfloat16 [1024, 3, 1024], P(None, None, 'tensor'), may hold values from -0.1875 to 0.1875
- qv_bias: float32 [2, 1024], P(None, 'tensor'), may hold values from -1.5 to 1.5
- proj_weight: bfloat16 [1024, 1024], P('tensor'), may hold values from -1.5 to 1.5
- proj_bias: float32 [1024], replicated, may hold values from -1.5 to 1.5
- norm2_gain: float32 [1024], replicated, may hold values from 0.25 to 1.75
- norm2_shift: float32 [1024], replicated, may hold values from -1.5 to 1.5
- up_weight: bfloat16 [1024, 4096], P(None, 'tensor'), may hold values from -0.1875 to 0.1875
- up_bias: float32 [4096], P('tensor'), may hold values from -1.5 to 1.5
- down_weight: bfloat16 [4096, 1024], P('tensor'), may hold values from -0.09375 to 0.09375
- down_bias: float32 [1024], replicated, may hold values from -1.5 to 1.5
- adapt_qkv_in: bfloat16 [1024, 128], replicated, may hold values from -0.1875 to 0.1875
- adapt_qkv_out: bfloat16 [128, 3, 1024], P(None, None, 'tensor'), may hold values from -0.75 to 0.75
- adapt_proj_in: bfloat16 [1024, 128], P('tensor'), may hold values from -0.75 to 0.75
- adapt_proj_out: bfloat16 [128, 1024], replicated, may hold values from -0.75 to 0.75
- adapt_up_in: bfloat16 [1024, 128], replicated, may hold values from -0.1875 to 0.1875
- adapt_up_out: bfloat16 [128, 4096], P(None, 'tensor'), may hold values from -0.75 to 0.75
- adapt_down_in: bfloat16 [4096, 128], P('tensor'), may hold values from -0.09375 to 0.09375
- adapt_down_out: bfloat16 [128, 1024], replicated, may hold values from -0.75 to 0.75
Outputs:
- result: float32 [8192, 1024], P(('dp', 'tensor'))
- grad_input: float32 [8192, 1024], P(('dp', 'tensor'))
- grad_qkv_in: float32 [1024, 128], replicated
- grad_qkv_out: float32 [128, 3, 1024], P(None, None, 'tensor')
- grad_proj_in: float32 [1024, 128], P('tensor')
- grad_proj_out: float32 [128, 1024], replicated
- grad_up_in: float32 [1024, 128], replicated
- grad_up_out: float32 [128, 4096], P(None, 'tensor')
- grad_down_in: float32 [4096, 128], P('tensor')
- grad_down_out: float32 [128, 1024], replicated
Inputs may be any that keep to these rules, and one draw needn't show every extreme that they name: `lengths`: in every group one sequence has exactly 512 valid tokens; the others have at least 512 // 8 (and at least one). `order`: each row is a permutation of the group's 1024 stored rows.
All inputs are finite; a program needn't handle non-finite values.
Results may differ from a plain program's by a relative error of at most 0.023.
Values may be sent and summed in bfloat16 or wider, within the bound.
No kernel may reach another device: no remote copies, remote signals or barrier semaphores. Data moves between devices by JAX's collectives and lax.ppermute only.
A program may use at most 128 MiB of HBM per device.

v0:
```python
import math
import jax
import jax.numpy as jnp
from jax import lax
from jax.sharding import PartitionSpec as P

D = 1024
HD = 64
RANK = 16
EPSILON = 1e-05
NEGATIVE = -1000000000.0


def layer_norm(values, gain, shift):
    centre = values - jnp.mean(values, -1, keepdims=True)
    spread = jnp.mean(centre * centre, -1, keepdims=True)
    return centre * lax.rsqrt(spread + EPSILON) * gain + shift


def matmul(left, right):
    return jnp.dot(left, right, preferred_element_type=jnp.float32)


def matmul_back(left, right):
    return lax.dot_general(
        left, right, (((1,), (1,)), ((), ())), preferred_element_type=jnp.float32
    )


def matmul_over(left, right):
    return lax.dot_general(
        left, right, (((0,), (0,)), ((), ())), preferred_element_type=jnp.float32
    )


def gelu_tanh(values):
    return jax.nn.gelu(values, approximate=True)


def block_scores(queries, keys, query_start, length):
    scale = 1.0 / math.sqrt(HD)
    scores = jnp.einsum("qhc,khc->hqk", queries, keys, preferred_element_type=jnp.float32) * scale
    query_pos = query_start + jnp.arange(queries.shape[0], dtype=jnp.int32)
    key_pos = jnp.arange(keys.shape[0], dtype=jnp.int32)
    allowed = (key_pos[None, :] <= query_pos[:, None]) & (key_pos[None, :] < length)
    return jnp.where(allowed[None], scores, NEGATIVE)


def attention_forward(qkv_seq, lengths_row, seq_len):
    group_rows = qkv_seq.shape[0]
    heads_here = qkv_seq.shape[2] // HD
    block_rows = min(512, seq_len)
    per_seq = seq_len // block_rows
    split = qkv_seq.reshape(group_rows, 3, heads_here, HD)

    def one_block(block_id):
        seq_id = block_id // per_seq
        query_start = block_id % per_seq * block_rows
        base = seq_id * seq_len
        queries = lax.dynamic_slice_in_dim(split[:, 0], base + query_start, block_rows, 0)
        keys = lax.dynamic_slice_in_dim(split[:, 1], base, seq_len, 0)
        values = lax.dynamic_slice_in_dim(split[:, 2], base, seq_len, 0)
        scores = block_scores(queries, keys, query_start, lengths_row[seq_id])
        top = jnp.max(scores, -1, keepdims=True)
        weights = jnp.exp(scores - top)
        total = jnp.sum(weights, -1, keepdims=True)
        probs = (weights / total).astype(jnp.bfloat16)
        attended = jnp.einsum("hqk,khc->qhc", probs, values, preferred_element_type=jnp.float32)
        return (attended.reshape(block_rows, heads_here * HD), (top + jnp.log(total))[..., 0])

    blocks = group_rows // block_rows
    outputs, log_totals = lax.map(one_block, jnp.arange(blocks, dtype=jnp.int32))
    return (outputs.reshape(group_rows, heads_here * HD), log_totals)


def attention_backward(qkv_seq, grad_seq, log_totals, lengths_row, seq_len):
    group_rows = qkv_seq.shape[0]
    heads_here = qkv_seq.shape[2] // HD
    block_rows = min(512, seq_len)
    per_seq = seq_len // block_rows
    seqs = group_rows // seq_len
    scale = 1.0 / math.sqrt(HD)
    split = qkv_seq.reshape(group_rows, 3, heads_here, HD)
    grad_split = grad_seq.reshape(group_rows, heads_here, HD)

    def one_block(block_id):
        seq_id = block_id // per_seq
        query_start = block_id % per_seq * block_rows
        base = seq_id * seq_len
        queries = lax.dynamic_slice_in_dim(split[:, 0], base + query_start, block_rows, 0)
        keys = lax.dynamic_slice_in_dim(split[:, 1], base, seq_len, 0)
        values = lax.dynamic_slice_in_dim(split[:, 2], base, seq_len, 0)
        grad_block = lax.dynamic_slice_in_dim(grad_split, base + query_start, block_rows, 0)
        scores = block_scores(queries, keys, query_start, lengths_row[seq_id])
        probs = jnp.exp(scores - log_totals[block_id][..., None])
        grad_probs = jnp.einsum(
            "qhc,khc->hqk", grad_block, values, preferred_element_type=jnp.float32
        )
        centre = jnp.sum(probs * grad_probs, -1, keepdims=True)
        grad_raw = (probs * (grad_probs - centre) * scale).astype(jnp.bfloat16)
        grad_query = jnp.einsum("hqk,khc->qhc", grad_raw, keys, preferred_element_type=jnp.float32)
        grad_key = jnp.einsum("hqk,qhc->khc", grad_raw, queries, preferred_element_type=jnp.float32)
        grad_value = jnp.einsum(
            "hqk,qhc->khc",
            probs.astype(jnp.bfloat16),
            grad_block,
            preferred_element_type=jnp.float32,
        )
        return (grad_query, grad_key, grad_value)

    blocks = group_rows // block_rows
    grad_query, grad_key, grad_value = lax.map(one_block, jnp.arange(blocks, dtype=jnp.int32))
    width_here = heads_here * HD
    grad_query = grad_query.reshape(group_rows, width_here)
    grad_key = jnp.sum(grad_key.reshape(seqs, per_seq, seq_len, width_here), axis=1).reshape(
        group_rows, width_here
    )
    grad_value = jnp.sum(grad_value.reshape(seqs, per_seq, seq_len, width_here), axis=1).reshape(
        group_rows, width_here
    )
    return jnp.stack([grad_query, grad_key, grad_value], 1)


def body(
    tokens,
    cotangent,
    lengths,
    order,
    adapter_ids,
    norm1_gain,
    norm1_shift,
    qkv_weight,
    qv_bias,
    proj_weight,
    proj_bias,
    norm2_gain,
    norm2_shift,
    up_weight,
    up_bias,
    down_weight,
    down_bias,
    adapt_qkv_in,
    adapt_qkv_out,
    adapt_proj_in,
    adapt_proj_out,
    adapt_up_in,
    adapt_up_out,
    adapt_down_in,
    adapt_down_out,
):
    own_rows = tokens.shape[0]
    order_row = order[0]
    lengths_row = lengths[0]
    ids_row = adapter_ids[0]
    group_rows = order_row.shape[0]
    seqs = lengths_row.shape[0]
    seq_len = group_rows // seqs
    adapt_cols = adapt_qkv_in.shape[1]
    rank_index = lax.axis_index("tensor")
    inverse = (
        jnp.zeros((group_rows,), jnp.int32)
        .at[order_row]
        .set(jnp.arange(group_rows, dtype=jnp.int32))
    )
    seq_of = inverse // seq_len
    adapter_of = jnp.sum(
        jnp.where(
            seq_of[:, None] == jnp.arange(seqs, dtype=jnp.int32)[None, :], ids_row[None, :], 0
        ),
        axis=1,
    )
    group_mask = (
        jnp.arange(adapt_cols, dtype=jnp.int32)[None, :] // RANK == adapter_of[:, None]
    ).astype(jnp.float32)
    own_mask = lax.dynamic_slice_in_dim(group_mask, rank_index * own_rows, own_rows, 0)
    bias_three = jnp.stack([qv_bias[0], jnp.zeros_like(qv_bias[0]), qv_bias[1]])
    proj_joined = jnp.concatenate([proj_weight, adapt_proj_in], 1)
    down_joined = jnp.concatenate([down_weight, adapt_down_in], 1)
    up_joined = jnp.concatenate([up_weight, adapt_up_out], 0)
    qkv_joined = jnp.concatenate([qkv_weight, adapt_qkv_out], 0)

    def project_qkv(rows_all, lowrank_all):
        value = jnp.einsum("rd,dkc->rkc", rows_all, qkv_weight, preferred_element_type=jnp.float32)
        value = value + jnp.einsum(
            "ra,akc->rkc", lowrank_all, adapt_qkv_out, preferred_element_type=jnp.float32
        )
        return (value + bias_three[None]).astype(jnp.bfloat16)

    def project_up(rows_all, lowrank_all):
        return matmul(rows_all, up_weight) + matmul(lowrank_all, adapt_up_out) + up_bias

    inputs = tokens.astype(jnp.float32)
    normed1 = layer_norm(inputs, norm1_gain, norm1_shift).astype(jnp.bfloat16)
    low1 = (matmul(normed1, adapt_qkv_in) * own_mask).astype(jnp.bfloat16)
    normed1_all, low1_small = (
        lax.all_gather(normed1, "tensor", axis=0, tiled=True),
        lax.all_gather(low1, "tensor", axis=0, tiled=True),
    )
    low1_all = low1_small
    qkv_arr = project_qkv(normed1_all, low1_all)
    qkv_seq = jnp.take(qkv_arr, order_row, axis=0)
    attended_seq, log_totals = attention_forward(qkv_seq, lengths_row, seq_len)
    attended = jnp.take(attended_seq.astype(jnp.bfloat16), inverse, axis=0)
    rows = attended
    mask_rows = group_mask
    part = matmul(rows, proj_joined)
    summed_attn = lax.psum_scatter(
        jnp.concatenate([part[:, :D], part[:, D:] * mask_rows], 1).astype(jnp.bfloat16),
        "tensor",
        scatter_dimension=0,
        tiled=True,
    ).astype(jnp.float32)
    proj_low = summed_attn[:, D:].astype(jnp.bfloat16)
    mid = inputs + summed_attn[:, :D] + matmul(proj_low, adapt_proj_out) + proj_bias
    normed2 = layer_norm(mid, norm2_gain, norm2_shift).astype(jnp.bfloat16)
    low2 = (matmul(normed2, adapt_up_in) * own_mask).astype(jnp.bfloat16)
    normed2_all, low2_small = (
        lax.all_gather(normed2, "tensor", axis=0, tiled=True),
        lax.all_gather(low2, "tensor", axis=0, tiled=True),
    )
    low2_all = low2_small
    upper = project_up(normed2_all, low2_all)
    active = gelu_tanh(upper).astype(jnp.bfloat16)
    rows = active
    mask_rows = group_mask
    part = matmul(rows, down_joined)
    summed_mlp = lax.psum_scatter(
        jnp.concatenate([part[:, :D], part[:, D:] * mask_rows], 1).astype(jnp.bfloat16),
        "tensor",
        scatter_dimension=0,
        tiled=True,
    ).astype(jnp.float32)
    down_low = summed_mlp[:, D:].astype(jnp.bfloat16)
    result = mid + summed_mlp[:, :D] + matmul(down_low, adapt_down_out) + down_bias
    grad_mlp = cotangent.astype(jnp.bfloat16)
    grad_down_low = (matmul_back(grad_mlp, adapt_down_out) * own_mask).astype(jnp.bfloat16)
    grad_down_out_part = matmul_over(down_low, grad_mlp)
    grad_mlp_all, grad_down_small = (
        lax.all_gather(grad_mlp, "tensor", axis=0, tiled=True),
        lax.all_gather(grad_down_low, "tensor", axis=0, tiled=True),
    )
    normed2_again, low2_again_small = (
        lax.all_gather(normed2, "tensor", axis=0, tiled=True),
        lax.all_gather(low2, "tensor", axis=0, tiled=True),
    )
    upper = project_up(normed2_again, low2_again_small)
    active = gelu_tanh(upper).astype(jnp.bfloat16)
    low2_all = low2_again_small
    grad_active = matmul_back(grad_mlp_all, down_weight) + matmul_back(
        grad_down_small, adapt_down_in
    )
    grad_down_in_part = matmul_over(active, grad_down_small)
    gelu_value, gelu_pull = jax.vjp(gelu_tanh, upper)
    grad_upper = gelu_pull(grad_active)[0].astype(jnp.bfloat16)
    grad_up_out_part = matmul_over(low2_all, grad_upper)
    rows = grad_upper
    part = matmul_back(rows, up_joined)
    summed_up = lax.psum_scatter(
        jnp.concatenate([part[:, :D], part[:, D:]], 1).astype(jnp.bfloat16),
        "tensor",
        scatter_dimension=0,
        tiled=True,
    ).astype(jnp.float32)
    grad_low2 = (summed_up[:, D:] * own_mask).astype(jnp.bfloat16)
    grad_up_in_part = matmul_over(normed2, grad_low2)
    grad_normed2 = summed_up[:, :D] + matmul_back(grad_low2, adapt_up_in)
    norm2_value, norm2_pull = jax.vjp(
        lambda values: layer_norm(values, norm2_gain, norm2_shift), mid
    )
    grad_mid = cotangent + norm2_pull(grad_normed2)[0]
    grad_attn = grad_mid.astype(jnp.bfloat16)
    grad_proj_low = (matmul_back(grad_attn, adapt_proj_out) * own_mask).astype(jnp.bfloat16)
    grad_proj_out_part = matmul_over(proj_low, grad_attn)
    grad_attn_all, grad_proj_small = (
        lax.all_gather(grad_attn, "tensor", axis=0, tiled=True),
        lax.all_gather(grad_proj_low, "tensor", axis=0, tiled=True),
    )
    grad_attended = matmul_back(grad_attn_all, proj_weight) + matmul_back(
        grad_proj_small, adapt_proj_in
    )
    grad_proj_in_part = matmul_over(attended, grad_proj_small)
    grad_attended_seq = jnp.take(grad_attended, order_row, axis=0).astype(jnp.bfloat16)
    normed1_again, low1_again_small = (
        lax.all_gather(normed1, "tensor", axis=0, tiled=True),
        lax.all_gather(low1, "tensor", axis=0, tiled=True),
    )
    qkv_seq = jnp.take(project_qkv(normed1_again, low1_again_small), order_row, axis=0)
    low1_all = low1_again_small
    grad_qkv_seq = attention_backward(qkv_seq, grad_attended_seq, log_totals, lengths_row, seq_len)
    grad_qkv = jnp.take(grad_qkv_seq.astype(jnp.bfloat16), inverse, axis=0)
    grad_qkv_out_part = jnp.einsum(
        "ra,rkc->akc", low1_all, grad_qkv, preferred_element_type=jnp.float32
    )
    rows = grad_qkv
    part = jnp.einsum("rkc,dkc->rd", rows, qkv_joined, preferred_element_type=jnp.float32)
    summed_qkv = lax.psum_scatter(
        jnp.concatenate([part[:, :D], part[:, D:]], 1).astype(jnp.bfloat16),
        "tensor",
        scatter_dimension=0,
        tiled=True,
    ).astype(jnp.float32)
    grad_low1 = (summed_qkv[:, D:] * own_mask).astype(jnp.bfloat16)
    grad_qkv_in_part = matmul_over(normed1, grad_low1)
    grad_normed1 = summed_qkv[:, :D] + matmul_back(grad_low1, adapt_qkv_in)
    norm1_value, norm1_pull = jax.vjp(
        lambda values: layer_norm(values, norm1_gain, norm1_shift), inputs
    )
    grad_input = grad_mid + norm1_pull(grad_normed1)[0]
    wide = lax.psum(
        (grad_qkv_in_part, grad_proj_out_part, grad_up_in_part, grad_down_out_part),
        ("dp", "tensor"),
    )
    narrow = (
        lax.psum(grad_qkv_out_part.astype(jnp.bfloat16), "dp").astype(jnp.float32),
        lax.psum(grad_proj_in_part.astype(jnp.bfloat16), "dp").astype(jnp.float32),
        lax.psum(grad_up_out_part.astype(jnp.bfloat16), "dp").astype(jnp.float32),
        lax.psum(grad_down_in_part.astype(jnp.bfloat16), "dp").astype(jnp.float32),
    )
    return (
        result,
        grad_input,
        wide[0],
        narrow[0],
        narrow[1],
        wide[1],
        wide[2],
        narrow[2],
        narrow[3],
        wide[3],
    )


def solution(mesh):
    in_specs = (
        P(("dp", "tensor"), None),
        P(("dp", "tensor"), None),
        P("dp", None),
        P("dp", None),
        P("dp", None),
        P(),
        P(),
        P(None, None, "tensor"),
        P(None, "tensor"),
        P("tensor", None),
        P(),
        P(),
        P(),
        P(None, "tensor"),
        P("tensor"),
        P("tensor", None),
        P(),
        P(),
        P(None, None, "tensor"),
        P("tensor", None),
        P(),
        P(),
        P(None, "tensor"),
        P("tensor", None),
        P(),
    )
    out_specs = (
        P(("dp", "tensor"), None),
        P(("dp", "tensor"), None),
        P(),
        P(None, None, "tensor"),
        P("tensor", None),
        P(),
        P(),
        P(None, "tensor"),
        P("tensor", None),
        P(),
    )
    return jax.shard_map(body, mesh=mesh, in_specs=in_specs, out_specs=out_specs, check_vma=False)
```

profile of v0, /device:TPU:0, one launch (start us, length us, event | category | flops | bytes accessed | tf_op | source)
XLA Modules:
  0.0 638.7 jit_solution(10005724395536461428)
XLA Ops:
  9.8 2.1 fusion.106
  12.8 4.3 scatter_custom_fusion
  20.2 8.9 %all_gather.29 = bf16[1024,128]{1,0:T(8,128)(2,1)S(1)} all-gather(bf16[256,128]{1,0:T(8,128)(2,1)S(1)} %fusion.97), channel_id=1, replica_groups=mesh['dp'=8,'tensor'=4] {'tensor'}, dimensions={0}, use_global_device_ids=true | all-gather | bytes 327680 | tf_op jit(solution)/shard_map/all_gather | solution.py:197
  31.9 6.9 %all-gather.5.cloned.1.call-done = bf16[1024,1024]{1,0:T(8,128)(2,1)} async-done(((bf16[256,1024]{1,0:T(8,128)(2,1)}), bf16[1024,1024]{1,0:T(8,128)(2,1)}) %all-gather.5.cloned.1.call-update) | async-done | bytes 2097168 | tf_op jit(solution)/shard_map/all_gather | solution.py:196
  38.8 3.8 fusion.84
  43.3 2.7 copy.65
  46.0 10.1 %gather_fusion.2 = bf16[1024,3,256]{2,1,0:T(4,128)(2,1)} fusion(bf16[1024,3,256]{2,1,0:T(4,128)(2,1)} %copy.65, s32[1024]{0:T(1024)S(1)} %fusion.129), kind=kCustom, calls=%fused_computation.clone | custom fusion | bytes 3149824 | tf_op jit(solution)/shard_map/jit(_take)/gather | solution.py:201
  56.1 6.3 broadcast_select_fusion.1
  62.4 2.9 copy.66
  65.3 15.9 %while.32 = (s32[]{:T(128)}, bf16[2,512,256]{1,2,0:T(8,128)(2,1)S(1)}, f32[2,4,512]{2,1,0:T(4,128)S(1)}, bf16[1024,3,4,64]{0,3,2,1:T(8,128)(2,1)S(1)}, s32[2]{0:...) while((s32[]{:T(128)}, ...), condition=%wide.region_7.9_spmd, body=%wide.region_4.8_spmd.sunk | while | flops 281541120 | bytes 18417900 | solution.py:72
  81.4 4.4 gather_fusion
  85.9 1.8 fusion.108
  91.6 32.2 %reduce-scatter.5.cloned.1.call-done = bf16[256,1152]{1,0:T(8,128)(2,1)} async-done(((bf16[1024,1152]{1,0:T(8,128)(2,1)}), bf16[256,1152]{1,0:T(8,128)(2,1)}) %reduce-scatter.5.cloned.1.call-update) | async-done | bytes 589840 | tf_op jit(solution)/shard_map/reduce_scatter | solution.py:207
  125.7 1.7 add_convert_fusion.1
  129.0 6.4 %all_gather.33 = bf16[1024,128]{1,0:T(8,128)(2,1)} all-gather(bf16[256,128]{1,0:T(8,128)(2,1)S(1)} %fusion.99), channel_id=1, replica_groups=mesh['dp'=8,'tensor'=4] {'tensor'}, dimensions={0}, use_global_device_ids=true | all-gather | bytes 327680 | tf_op jit(solution)/shard_map/all_gather | solution.py:240
  135.4 13.3 %all-gather.9.cloned.1.call-done = bf16[1024,1024]{1,0:T(8,128)(2,1)} async-done(((bf16[256,1024]{1,0:T(8,128)(2,1)}), bf16[1024,1024]{1,0:T(8,128)(2,1)}) %all-gather.9.cloned.1.call-update) | async-done | bytes 2097168 | tf_op jit(solution)/shard_map/all_gather | solution.py:239
  148.7 6.6 %fusion.153 = f32[1024,1024]{1,0:T(8,128)} fusion(bf16[1024,1024]{1,0:T(8,128)(2,1)} %all-gather.9.cloned.1.call-done, bf16[1024,1024]{1,0:T(8,128)(2,1)} %param.46), kind=kOutput, calls=%fused_computation.219 | convolution fusion | flops 2147483648 | bytes 8388608 | tf_op jit(solution)/shard_map/dot_general | solution.py:25
  155.6 5.8 all_gather.31
  161.4 12.0 %all-gather.7.cloned.1.call-done = bf16[1024,1024]{1,0:T(8,128)(2,1)} async-done(((bf16[256,1024]{1,0:T(8,128)(2,1)}), bf16[1024,1024]{1,0:T(8,128)(2,1)}) %all-gather.7.cloned.1.call-update) | async-done | bytes 2097168 | tf_op jit(solution)/shard_map/all_gather | solution.py:218
  173.4 4.6 fusion.152
  178.7 2.1 copy-done.18
  181.8 3.2 fusion.76
  186.5 4.2 convolution_convert_fusion
  190.7 33.2 %reduce-scatter.9.cloned.1.call-done = bf16[256,1152]{1,0:T(8,128)(2,1)} async-done(((bf16[1024,1152]{1,0:T(8,128)(2,1)}), bf16[256,1152]{1,0:T(8,128)(2,1)}) %reduce-scatter.9.cloned.1.call-update) | async-done | bytes 589840 | tf_op jit(solution)/shard_map/reduce_scatter | solution.py:258
  229.6 6.5 %fusion.77 = bf16[1024,1152]{1,0:T(8,128)(2,1)S(1)} fusion(bf16[1024,128]{1,0:T(8,128)(2,1)S(1)} %copy-done.64, bf16[1024,1024]{1,0:T(8,128)(2,1)} %param.46, f32[1024,1024]{1,0:T(8,128)} %copy-done.18), kind=kOutput, calls=%fused_computation.87 | convolution fusion | flops 2430074880 | bytes 8912896 | tf_op jit(solution)/shard_map/dot_general | solution.py:21
  240.9 4.8 convolution_convert_fusion.1
  246.1 6.3 all_gather.35
  252.3 2.2 convolution_convert_fusion.4
  254.6 2.4 fusion.154
  257.4 5.5 gather_fusion.1
  262.9 2.1 copy.68
  266.1 62.1 %while.33 = (s32[]{:T(128)}, bf16[2,512,4,64]{1,3,2,0:T(8,128)(2,1)}, bf16[2,512,4,64]{1,3,2,0:T(8,128)(2,1)}, bf16[2,512,4,64]{1,3,2,0:T(8,128)(2,1)}, bf16[102...) while((s32[]{:T(128)}, ...), condition=%wide.region_17.19_spmd, body=%wide.region_15.18_spmd.sunk | while | flops 686298624 | bytes 57437636 | solution.py:112
  271.6 2.8 fusion.230
  274.4 3.3 subtract_exponential_fusion.3
  277.6 7.9 %fusion.232 = bf16[2,512,4,64]{1,3,2,0:T(8,128)(2,1)} fusion(bf16[2,512,4,64]{1,3,2,0:T(8,128)(2,1)} %get-tuple-element.493, s32[]{:T(128)S(6)} %copy.112, f32[4,512,512]{1,2,0:T(8,128)} %subtract_exponential_fusion.3, f32[4,512,512]{1,2,0:T(8,128)} %fusion.230, bf16[1024,1,4,64]{0,3,2,1:T(8,128)(2,1)} %copy-done.5, s32[]{:T(128)S(6)} %select_n.203), kind=kOutput, calls=%fused_computation.43.clone.1 | convolution fusion | flops 139463168 | bytes 17563656 | tf_op jit(solution)/shard_map/while/body/eval_jaxpr/hqk,qhc->khc/dot_general | solution.py:102
  285.6 8.0 %fusion.231 = bf16[2,512,4,64]{1,3,2,0:T(8,128)(2,1)} fusion(bf16[2,512,4,64]{1,3,2,0:T(8,128)(2,1)} %get-tuple-element.492, s32[]{:T(128)S(6)} %copy.112, f32[4,512,512]{1,2,0:T(8,128)} %subtract_exponential_fusion.3, f32[4,512,512]{1,2,0:T(8,128)} %fusion.230, bf16[1024,1,4,64]{0,3,2,1:T(8,128)(2,1)} %copy-done.4, s32[]{:T(128)S(6)} %select_n.203), kind=kOutput, calls=%fused_computation.41.clone.1 | convolution fusion | flops 139463168 | bytes 17563656 | tf_op jit(solution)/shard_map/while/body/eval_jaxpr/hqk,khc->qhc/dot_general | solution.py:101
  293.6 3.7 fusion.233
  302.7 2.8 fusion.230
  305.4 3.3 subtract_exponential_fusion.3
  308.7 7.9 %fusion.232 = bf16[2,512,4,64]{1,3,2,0:T(8,128)(2,1)} fusion(bf16[2,512,4,64]{1,3,2,0:T(8,128)(2,1)} %get-tuple-element.493, s32[]{:T(128)S(6)} %copy.112, f32[4,512,512]{1,2,0:T(8,128)} %subtract_exponential_fusion.3, f32[4,512,512]{1,2,0:T(8,128)} %fusion.230, bf16[1024,1,4,64]{0,3,2,1:T(8,128)(2,1)} %copy-done.5, s32[]{:T(128)S(6)} %select_n.203), kind=kOutput, calls=%fused_computation.43.clone.1 | convolution fusion | flops 139463168 | bytes 17563656 | tf_op jit(solution)/shard_map/while/body/eval_jaxpr/hqk,qhc->khc/dot_general | solution.py:102
  316.6 8.0 %fusion.231 = bf16[2,512,4,64]{1,3,2,0:T(8,128)(2,1)} fusion(bf16[2,512,4,64]{1,3,2,0:T(8,128)(2,1)} %get-tuple-element.492, s32[]{:T(128)S(6)} %copy.112, f32[4,512,512]{1,2,0:T(8,128)} %subtract_exponential_fusion.3, f32[4,512,512]{1,2,0:T(8,128)} %fusion.230, bf16[1024,1,4,64]{0,3,2,1:T(8,128)(2,1)} %copy-done.4, s32[]{:T(128)S(6)} %select_n.203), kind=kOutput, calls=%fused_computation.41.clone.1 | convolution fusion | flops 139463168 | bytes 17563656 | tf_op jit(solution)/shard_map/while/body/eval_jaxpr/hqk,khc->qhc/dot_general | solution.py:101
  324.6 3.7 fusion.233
  328.3 2.4 copy.85
  330.6 3.9 reshape.388
  334.5 2.3 copy.83
  336.9 4.8 reshape.386
  343.0 4.8 reshape.387
  347.8 5.8 pad_maximum_fusion.2
  353.6 10.2 %gather_fusion.3 = bf16[1024,3,256]{2,1,0:T(4,128)(2,1)} fusion(bf16[1024,3,256]{2,1,0:T(4,128)(2,1)} %pad_maximum_fusion.2, s32[1024]{0:T(1024)S(1)} %copy-done.40), kind=kCustom, calls=%fused_computation.1.clone | custom fusion | bytes 3149824 | tf_op jit(solution)/shard_map/jit(_take)/gather | solution.py:290
  363.8 5.3 broadcast_select_fusion
  371.9 5.7 bitcast_convert_fusion
  377.7 1.9 fusion.122
  379.6 1.9 fusion.119
  381.6 2.0 fusion.132
  383.6 2.3 fusion.95
  386.0 61.0 %all-reduce.7.cloned.1.call-done = (bf16[128,3,256]{2,0,1:T(8,128)(2,1)}, bf16[256,128]{1,0:T(8,128)(2,1)}, bf16[128,1024]{1,0:T(8,128)(2,1)}, bf16[1024,128]{1,0:T(8,128)(2,1)}) async-done(((bf16[128,3,256]{2,0,1:T(8,128)(2,1)}, bf16[256,128]{1,0:T(8,128)(2,1)}, bf16[128,1024]{1,0:T(8,128)(2,1)}, bf16[1024,128]{1,0:T(8,128)(2,1)}), (bf16[128,3,256]{2,0,1:T(8,128)(2,1)}, bf16[256,128]{1,0:T(8,128)(2,1)}, ...) | async-done | bytes 786448 | tf_op jit(solution)/shard_map/psum | solution.py:314
  450.2 1.8 convert_element_type.148
  451.9 1.8 convert_element_type.150
  453.7 27.9 %reduce-scatter.11.cloned.1.call-done = bf16[256,1152]{1,0:T(8,128)(2,1)} async-done(((bf16[1024,1152]{1,0:T(8,128)(2,1)}), bf16[256,1152]{1,0:T(8,128)(2,1)}) %reduce-scatter.11.cloned.1.call-update) | async-done | bytes 589840 | tf_op jit(solution)/shard_map/reduce_scatter | solution.py:296
  489.3 134.8 %all-reduce.5.cloned.1.call-done = (f32[1024,128]{1,0:T(8,128)}, f32[128,1024]{1,0:T(8,128)}, f32[1024,128]{1,0:T(8,128)}, f32[128,1024]{1,0:T(8,128)}) async-done(((f32[1024,128]{1,0:T(8,128)}, f32[128,1024]{1,0:T(8,128)}, f32[1024,128]{1,0:T(8,128)}, f32[128,1024]{1,0:T(8,128)}), (f32[1024,128]{1,0:T(8,128)}, f32[128,1024]{1,0:T(8,128)}, f32[1024,128]{1,0:T(8,128)}, ...) | async-done | bytes 2097168 | tf_op jit(solution)/shard_map/psum | solution.py:309
  624.1 1.9 copy.137
  626.0 1.9 copy.138
  627.9 1.9 copy.139
  629.7 1.9 copy.140
  (261 shorter events, 63.9 us)
Async XLA Ops:
  7.2 148.1 %copy-start = (bf16[1024,128]{1,0:T(8,128)(2,1)S(1)}, bf16[1024,128]{1,0:T(8,128)(2,1)}, u32[]{:S(2)}) copy-start(bf16[1024,128]{1,0:T(8,128)(2,1)} %param.52) | copy-start | bytes 786436
  7.2 31.6 %all-gather.5.cloned.1.call-start = ((), (), s32[]{:S(2)}) async-start(), calls=%async_computation.4 | async-start | bytes 2621440 | tf_op jit(solution)/shard_map/all_gather | solution.py:196
  8.5 30.4 %copy-start.38 = (f32[256]{0:T(256)}, f32[256]{0:T(256)S(1)}, u32[]{:S(2)}) copy-start(f32[256]{0:T(256)S(1)} %broadcast_multiply_fusion.1) | copy-start | bytes 3076
  9.8 29.0 %copy-start.55 = (f32[256]{0:T(256)}, f32[256]{0:T(256)S(1)}, u32[]{:S(2)}) copy-start(f32[256]{0:T(256)S(1)} %fusion.103) | copy-start | bytes 3076
  9.8 29.0 %copy-start.46 = (f32[256]{0:T(256)}, f32[256]{0:T(256)S(1)}, u32[]{:S(2)}) copy-start(f32[256]{0:T(256)S(1)} %fusion.138) | copy-start | bytes 3076
  12.0 111.8 %reduce-scatter.5.cloned.1.call-start = ((), (), s32[]{:S(2)}) async-start(), calls=%async_computation.5 | async-start | bytes 2949120 | tf_op jit(solution)/shard_map/reduce_scatter | solution.py:207
  12.8 4.3 copy-start.44
  17.2 14.0 %copy-start.58 = (s32[128]{0:T(128)}, s32[128]{0:T(128)S(1)}, u32[]{:S(2)}) copy-start(s32[128]{0:T(128)S(1)} %and_select_fusion) | copy-start | bytes 1540
  18.5 24.1 %copy-start.36 = (s32[1024]{0:T(1024)}, s32[1024]{0:T(1024)S(1)}, u32[]{:S(2)}) copy-start(s32[1024]{0:T(1024)S(1)} %fusion.125) | copy-start | bytes 12292
  29.1 13.6 %copy-start.19 = (bf16[1024,128]{1,0:T(8,128)(2,1)}, bf16[1024,128]{1,0:T(8,128)(2,1)S(1)}, u32[]{:S(2)}) copy-start(bf16[1024,128]{1,0:T(8,128)(2,1)S(1)} %all_gather.29) | copy-start | bytes 786436
  31.2 24.9 %copy-start.49 = (pred[1024]{0:T(1024)(128)(4,1)}, pred[1024]{0:T(1024)(128)(4,1)S(1)}, u32[]{:S(2)}) copy-start(pred[1024]{0:T(1024)(128)(4,1)S(1)} %compare_and_fusion) | copy-start | bytes 3076
  31.9 10.8 %copy-start.34 = (bf16[128,3,256]{2,0,1:T(8,128)(2,1)S(1)}, bf16[128,3,256]{2,0,1:T(8,128)(2,1)}, u32[]{:S(2)}) copy-start(bf16[128,3,256]{2,0,1:T(8,128)(2,1)} %param.49) | copy-start | bytes 589828
  56.1 9.2 %copy-start.65 = (s32[1,2]{1,0:T(1,128)S(1)}, s32[1,2]{1,0:T(1,128)}, u32[]{:S(2)}) copy-start(s32[1,2]{1,0:T(1,128)} %param.33) | copy-start | bytes 28
  81.2 4.7 copy-start.29
  88.9 34.9 %copy-start.2 = (bf16[256,1024]{1,0:T(8,128)(2,1)S(1)}, bf16[256,1024]{1,0:T(8,128)(2,1)}, u32[]{:S(2)}) copy-start(bf16[256,1024]{1,0:T(8,128)(2,1)} %param.31) | copy-start | bytes 1572868
  90.6 58.1 %all-gather.9.cloned.1.call-start = ((), (), s32[]{:S(2)}) async-start(), calls=%async_computation.8 | async-start | bytes 2621440 | tf_op jit(solution)/shard_map/all_gather | solution.py:239
  91.6 81.8 %all-gather.7.cloned.1.call-start = ((), (), s32[]{:S(2)}) async-start(), calls=%async_computation.6 | async-start | bytes 2621440 | tf_op jit(solution)/shard_map/all_gather | solution.py:218
  127.5 96.4 %reduce-scatter.9.cloned.1.call-start = ((), (), s32[]{:S(2)}) async-start(), calls=%async_computation.9 | async-start | bytes 2949120 | tf_op jit(solution)/shard_map/reduce_scatter | solution.py:258
  135.4 19.9 %copy-start.15 = (bf16[256,1024]{1,0:T(8,128)(2,1)S(1)}, bf16[256,1024]{1,0:T(8,128)(2,1)}, u32[]{:S(2)}) copy-start(bf16[256,1024]{1,0:T(8,128)(2,1)} %add_convert_fusion.1) | copy-start | bytes 1572868
  161.3 16.6 %copy-start.31 = (bf16[128,1024]{1,0:T(8,128)(2,1)S(1)}, bf16[128,1024]{1,0:T(8,128)(2,1)}, u32[]{:S(2)}) copy-start(bf16[128,1024]{1,0:T(8,128)(2,1)} %param.53) | copy-start | bytes 786436
  173.4 4.6 copy-start.60
  178.0 2.9 copy-start.32
  178.0 2.9 copy-start.63
  178.0 3.9 copy-start.68
  181.8 4.6 copy-start.62
  190.7 35.7 %copy-start.57 = (f32[256]{0:T(256)S(1)}, f32[256]{0:T(256)}, u32[]{:S(2)}) copy-start(f32[256]{0:T(256)} %copy-done.56) | copy-start | bytes 3076
  190.7 35.8 %copy-start.42 = (f32[256]{0:T(256)S(1)}, f32[256]{0:T(256)}, u32[]{:S(2)}) copy-start(f32[256]{0:T(256)} %copy-done.41) | copy-start | bytes 3076
  190.7 35.8 %copy-start.54 = (f32[256]{0:T(256)S(1)}, f32[256]{0:T(256)}, u32[]{:S(2)}) copy-start(f32[256]{0:T(256)} %copy-done.53) | copy-start | bytes 3076
  190.7 63.9 %all-gather.11.cloned.1.call-start = ((), (), s32[]{:S(2)}) async-start(), calls=%async_computation.10 | async-start | bytes 2621440 | tf_op jit(solution)/shard_map/all_gather | solution.py:275
  223.9 4.0 copy-start.7
  225.1 3.8 copy-start.45
  226.4 3.2 copy-start.64
  228.9 150.7 %reduce-scatter.7.cloned.1.call-start = ((), (), s32[]{:S(2)}) async-start(), calls=%async_computation.7 | async-start | bytes 2949120 | tf_op jit(solution)/shard_map/reduce_scatter | solution.py:227
  240.9 4.9 copy-start.12
  240.9 4.9 copy-start.26
  245.7 201.2 %all-reduce.7.cloned.1.call-start = ((), (), s32[]{:S(2)}) async-start(), calls=%async_computation.13 | async-start | bytes 1572864 | tf_op jit(solution)/shard_map/psum | solution.py:314
  257.3 7.6 %copy-start.50 = (pred[1024]{0:T(1024)(128)(4,1)S(1)}, pred[1024]{0:T(1024)(128)(4,1)}, u32[]{:S(2)}) copy-start(pred[1024]{0:T(1024)(128)(4,1)} %copy-done.49) | copy-start | bytes 3076
  266.1 5.1 copy-start.66
  285.6 11.7 %copy-start.67 = (s32[2]{0:T(128)S(1)}, s32[2]{0:T(128)}, u32[]{:S(2)}) copy-start(s32[2]{0:T(128)} %copy-done.66) | copy-start | bytes 28 | tf_op jit(solution)/shard_map/while
  297.2 5.1 copy-start.66
  302.6 2.8 copy-start.4
  316.6 11.7 %copy-start.67 = (s32[2]{0:T(128)S(1)}, s32[2]{0:T(128)}, u32[]{:S(2)}) copy-start(s32[2]{0:T(128)} %copy-done.66) | copy-start | bytes 28 | tf_op jit(solution)/shard_map/while
  328.3 13.4 %copy-start.30 = (bf16[2,512,4,64]{1,3,2,0:T(8,128)(2,1)S(1)}, bf16[2,512,4,64]{1,3,2,0:T(8,128)(2,1)}, u32[]{:S(2)}) copy-start(bf16[2,512,4,64]{1,3,2,0:T(8,128)(2,1)} %get-tuple-element.261) | copy-start | bytes 1572868
  341.6 12.0 %copy-start.40 = (s32[1024]{0:T(1024)S(1)}, s32[1024]{0:T(1024)}, u32[]{:S(2)}) copy-start(s32[1024]{0:T(1024)} %get-tuple-element.326) | copy-start | bytes 12292
  347.8 16.0 %copy-start.48 = (pred[1024]{0:T(1024)(128)(4,1)S(1)}, pred[1024]{0:T(1024)(128)(4,1)}, u32[]{:S(2)}) copy-start(pred[1024]{0:T(1024)(128)(4,1)} %compare_and_fusion.1) | copy-start | bytes 3076
  353.6 16.8 %copy-start.20 = (bf16[1024,128]{1,0:T(8,128)(2,1)S(1)}, bf16[1024,128]{1,0:T(8,128)(2,1)}, u32[]{:S(2)}) copy-start(bf16[1024,128]{1,0:T(8,128)(2,1)} %copy-done.19) | copy-start | bytes 786436
  363.8 8.1 %copy-start.35 = (bf16[128,3,256]{2,0,1:T(8,128)(2,1)S(1)}, bf16[128,3,256]{2,0,1:T(8,128)(2,1)}, u32[]{:S(2)}) copy-start(bf16[128,3,256]{2,0,1:T(8,128)(2,1)} %param.49) | copy-start | bytes 589828
  371.5 6.1 copy-start.13
  371.6 8.1 %copy-start.11 = (bf16[256,1024]{1,0:T(8,128)(2,1)S(1)}, bf16[256,1024]{1,0:T(8,128)(2,1)}, u32[]{:S(2)}) copy-start(bf16[256,1024]{1,0:T(8,128)(2,1)} %convert_element_type.131) | copy-start | bytes 1572868
  371.6 110.1 %reduce-scatter.11.cloned.1.call-start = ((), (), s32[]{:S(2)}) async-start(), calls=%async_computation.11 | async-start | bytes 2949120 | tf_op jit(solution)/shard_map/reduce_scatter | solution.py:296
  377.6 4.0 copy-start.16
  377.6 6.0 copy-start.27
  377.6 6.0 copy-start.61
  377.6 246.5 %all-reduce.5.cloned.1.call-start = ((), (), s32[]{:S(2)}) async-start(), calls=%async_computation.12 | async-start | bytes 4194304 | tf_op jit(solution)/shard_map/psum | solution.py:309
  379.6 104.2 %copy-start.14 = (bf16[256,1024]{1,0:T(8,128)(2,1)S(1)}, bf16[256,1024]{1,0:T(8,128)(2,1)}, u32[]{:S(2)}) copy-start(bf16[256,1024]{1,0:T(8,128)(2,1)} %fusion.106) | copy-start | bytes 1572868
  386.0 99.1 %copy-start.3 = (bf16[256,1024]{1,0:T(8,128)(2,1)S(1)}, bf16[256,1024]{1,0:T(8,128)(2,1)}, u32[]{:S(2)}) copy-start(bf16[256,1024]{1,0:T(8,128)(2,1)} %param.31) | copy-start | bytes 1572868
  386.0 99.1 %copy-start.28 = (bf16[1024,128]{1,0:T(8,128)(2,1)S(1)}, bf16[1024,128]{1,0:T(8,128)(2,1)}, u32[]{:S(2)}) copy-start(bf16[1024,128]{1,0:T(8,128)(2,1)} %param.48) | copy-start | bytes 786436
  386.0 99.1 %copy-start.39 = (f32[256]{0:T(256)S(1)}, f32[256]{0:T(256)}, u32[]{:S(2)}) copy-start(f32[256]{0:T(256)} %copy-done.38) | copy-start | bytes 3076
  386.0 99.1 %copy-start.43 = (f32[1024]{0:T(1024)S(1)}, f32[1024]{0:T(1024)}, u32[]{:S(2)}) copy-start(f32[1024]{0:T(1024)} %param.36) | copy-start | bytes 12292
  450.2 37.3 %copy-start.47 = (f32[256]{0:T(256)S(1)}, f32[256]{0:T(256)}, u32[]{:S(2)}) copy-start(f32[256]{0:T(256)} %copy-done.46) | copy-start | bytes 3076
  453.7 34.1 %copy-start.8 = (f32[256,1024]{1,0:T(8,128)S(1)}, f32[256,1024]{1,0:T(8,128)}, u32[]{:S(2)}) copy-start(f32[256,1024]{1,0:T(8,128)} %param.32) | copy-start | bytes 3145732
  453.7 34.1 %copy-start.10 = (f32[256,1024]{1,0:T(8,128)S(1)}, f32[256,1024]{1,0:T(8,128)}, u32[]{:S(2)}) copy-start(f32[256,1024]{1,0:T(8,128)} %copy-done.9) | copy-start | bytes 3145732
  453.7 34.1 %copy-start.52 = (f32[256]{0:T(256)S(1)}, f32[256]{0:T(256)}, u32[]{:S(2)}) copy-start(f32[256]{0:T(256)} %copy-done.51) | copy-start | bytes 3076
  487.8 143.8 %copy-start.1 = (bf16[1024,128]{1,0:T(8,128)(2,1)S(1)}, bf16[1024,128]{1,0:T(8,128)(2,1)}, u32[]{:S(2)}) copy-start(bf16[1024,128]{1,0:T(8,128)(2,1)} %param.52) | copy-start | bytes 786436
  (19 other events, 35.3 us)
Sparse Core Ops, SparseCore 0:
  12.1 26.6 all-gather.4
  90.7 33.0 reduce-scatter.4
  126.0 22.5 all-gather.8
  150.7 22.5 all-gather.6
  190.8 33.0 reduce-scatter.8
  229.0 23.5 all-gather.10
  255.1 33.1 reduce-scatter.6
  371.7 75.2 all-reduce.6
  449.5 32.0 reduce-scatter.10
  489.2 134.8 all-reduce.4
where the time goes:
time: 643 us; the launch traced here: 639 us
  waiting for transfers between devices  321 us (50%)
  matrix products  123 us (19%)
  local copies, waits for them, and re-layouts  87.2 us (14%)
  other arithmetic  53.3 us (8%)
  blocking collectives  27.4 us (4%)
  between operations  15.3 us (2%)
  loops' own time  10.6 us (2%)
    psum x1, waiting for transfers between devices, body(): lax.psum((grad_qkv_in_part, grad_proj_out_part, grad_up_in_part, grad_dow...  135 us
    reduce_scatter x2, waiting for transfers between devices, body(): lax.psum_scatter(jnp.concatenate([part[:, :D], part[:, D:]], 1).astype(jn...  61 us
    psum x1, waiting for transfers between devices, body(): lax.psum(grad_qkv_out_part.astype(jnp.bfloat16), 'dp').astype(jnp.float32)  61 us
    reduce_scatter x2, waiting for transfers between devices, body(): lax.psum_scatter(jnp.concatenate([part[:, :D], part[:, D:] * mask_rows],...  32.2 us
    dot_general x9, matrix products, matmul_back(): lax.dot_general(left, right, (((1,), (1,)), ((), ())), preferred_element_...  21.5 us
    another operation x6, local copies, waits for them, and re-layouts, attention_backward(): return jnp.stack([grad_query, grad_key, grad_value], 1)  19.6 us
    dot_general x8, matrix products, matmul(): return jnp.dot(left, right, preferred_element_type=jnp.float32)  19.2 us
    unnamed x134, local copies, waits for them, and re-layouts  17.1 us
  transfers between devices with their start and end apart: 10, of which 8 were waited for; matrix products, arithmetic and copies ran while one was open for 28% of the time, Pallas kernels for 0%

commit v1 on v0

--- a/solution.py
+++ b/solution.py
@@ -307,8 +307,10 @@
     )
     grad_input = grad_mid + norm1_pull(grad_normed1)[0]
     wide = lax.psum(
-        (grad_qkv_in_part, grad_proj_out_part, grad_up_in_part, grad_down_out_part),
-        ("dp", "tensor"),
+        lax.psum(
+            (grad_qkv_in_part, grad_proj_out_part, grad_up_in_part, grad_down_out_part), "tensor"
+        ),
+        "dp",
     )
     narrow = (
         lax.psum(grad_qkv_out_part.astype(jnp.bfloat16), "dp").astype(jnp.float32),

time: 643 us -> 668 us (1.039)
  waiting for transfers between devices: 321 us -> 347 us
    psum x0 -> x1, waiting for transfers between devices: none -> 96.3 us  [body(): lax.psum(lax.psum((grad_qkv_in_part, grad_proj_out_part, grad_up_in_part,...]
    psum x1, waiting for transfers between devices: 135 us -> 42.3 us  [body(): lax.psum((grad_qkv_in_part, grad_proj_out_part, grad_up_in_part, grad_dow...]
    psum x1, waiting for transfers between devices: 61 us -> 77.9 us  [body(): lax.psum(grad_qkv_out_part.astype(jnp.bfloat16), 'dp').astype(jnp.float32)]
    unnamed x134 -> x150, local copies, waits for them, and re-layouts: 17.1 us -> 18 us
  transfers between devices with their start and end apart: 10 -> 11, of which waited for: 8 -> 10; matrix products, arithmetic and copies ran while one was open for 28% -> 26% of each run, Pallas kernels for 0% -> 0%
where the time goes in v1:
time: 668 us; the launch traced here: 663 us
  waiting for transfers between devices  347 us (52%)
  matrix products  121 us (18%)
  local copies, waits for them, and re-layouts  87.8 us (13%)
  other arithmetic  53.1 us (8%)
  blocking collectives  28.8 us (4%)
  between operations  15 us (2%)
  loops' own time  10.6 us (2%)
    psum x1, waiting for transfers between devices, body(): lax.psum(lax.psum((grad_qkv_in_part, grad_proj_out_part, grad_up_in_part,...  96.3 us
    psum x1, waiting for transfers between devices, body(): lax.psum(grad_qkv_out_part.astype(jnp.bfloat16), 'dp').astype(jnp.float32)  77.9 us
    reduce_scatter x2, waiting for transfers between devices, body(): lax.psum_scatter(jnp.concatenate([part[:, :D], part[:, D:]], 1).astype(jn...  60.5 us
    psum x1, waiting for transfers between devices, body(): lax.psum((grad_qkv_in_part, grad_proj_out_part, grad_up_in_part, grad_dow...  42.3 us
    reduce_scatter x2, waiting for transfers between devices, body(): lax.psum_scatter(jnp.concatenate([part[:, :D], part[:, D:] * mask_rows],...  32.2 us
    dot_general x9, matrix products, matmul_back(): lax.dot_general(left, right, (((1,), (1,)), ((), ())), preferred_element_...  20.7 us
    another operation x6, local copies, waits for them, and re-layouts, attention_backward(): return jnp.stack([grad_query, grad_key, grad_value], 1)  19.6 us
    dot_general x8, matrix products, matmul(): return jnp.dot(left, right, preferred_element_type=jnp.float32)  19.3 us
  transfers between devices with their start and end apart: 11, of which 10 were waited for; matrix products, arithmetic and copies ran while one was open for 26% of the time, Pallas kernels for 0%

profile of v1, /device:TPU:0, one launch (start us, length us, event | category | flops | bytes accessed | tf_op | source)
XLA Modules:
  0.0 663.1 jit_solution(13907715982622904005)
XLA Ops:
  9.8 2.1 fusion.106
  12.8 4.3 scatter_custom_fusion
  20.5 9.1 %all_gather.29 = bf16[1024,128]{1,0:T(8,128)(2,1)S(1)} all-gather(bf16[256,128]{1,0:T(8,128)(2,1)S(1)} %fusion.97), channel_id=1, replica_groups=mesh['dp'=8,'tensor'=4] {'tensor'}, dimensions={0}, use_global_device_ids=true | all-gather | bytes 327680 | tf_op jit(solution)/shard_map/all_gather | solution.py:197
  32.4 6.4 all-gather.5.cloned.1.call-done
  38.8 3.8 fusion.84
  44.6 8.7 %gather_fusion.2 = bf16[1024,3,256]{2,1,0:T(4,128)(2,1)} fusion(bf16[1024,3,256]{2,1,0:T(4,128)(2,1)S(1)} %copy.65, s32[1024]{0:T(1024)S(1)} %fusion.129), kind=kCustom, calls=%fused_computation.clone | custom fusion | bytes 3149824 | tf_op jit(solution)/shard_map/jit(_take)/gather | solution.py:201
  53.3 6.3 broadcast_select_fusion.1
  59.6 2.9 copy.66
  62.5 17.3 %while.32 = (s32[]{:T(128)}, bf16[2,512,256]{1,2,0:T(8,128)(2,1)}, f32[2,4,512]{2,1,0:T(4,128)S(1)}, bf16[1024,3,4,64]{0,3,2,1:T(8,128)(2,1)S(1)}, s32[2]{0:T(12...) while((s32[]{:T(128)}, bf16[2,512,256]{1,2,0:T(8,128)(2,1)}, ...), condition=%wide.region_7.9_spmd, body=%wide.region_4.8_spmd.sunk | while | flops 281541120 | bytes 18417900 | solution.py:72
  81.1 4.4 gather_fusion
  85.5 1.8 fusion.108
  91.3 32.2 %reduce-scatter.5.cloned.1.call-done = bf16[256,1152]{1,0:T(8,128)(2,1)} async-done(((bf16[1024,1152]{1,0:T(8,128)(2,1)}), bf16[256,1152]{1,0:T(8,128)(2,1)}) %reduce-scatter.5.cloned.1.call-update) | async-done | bytes 589840 | tf_op jit(solution)/shard_map/reduce_scatter | solution.py:207
  129.7 6.4 all_gather.33
  136.1 12.2 %all-gather.9.cloned.1.call-done = bf16[1024,1024]{1,0:T(8,128)(2,1)} async-done(((bf16[256,1024]{1,0:T(8,128)(2,1)}), bf16[1024,1024]{1,0:T(8,128)(2,1)}) %all-gather.9.cloned.1.call-update) | async-done | bytes 2097168 | tf_op jit(solution)/shard_map/all_gather | solution.py:239
  148.3 6.6 fusion.153
  155.2 5.8 all_gather.31
  161.0 12.0 %all-gather.7.cloned.1.call-done = bf16[1024,1024]{1,0:T(8,128)(2,1)} async-done(((bf16[256,1024]{1,0:T(8,128)(2,1)}), bf16[1024,1024]{1,0:T(8,128)(2,1)}) %all-gather.7.cloned.1.call-update) | async-done | bytes 2097168 | tf_op jit(solution)/shard_map/all_gather | solution.py:218
  173.0 4.6 fusion.152
  178.4 2.1 copy-done.19
  181.5 3.2 fusion.76
  186.1 4.2 convolution_convert_fusion
  190.4 33.2 %reduce-scatter.9.cloned.1.call-done = bf16[256,1152]{1,0:T(8,128)(2,1)} async-done(((bf16[1024,1152]{1,0:T(8,128)(2,1)}), bf16[256,1152]{1,0:T(8,128)(2,1)}) %reduce-scatter.9.cloned.1.call-update) | async-done | bytes 589840 | tf_op jit(solution)/shard_map/reduce_scatter | solution.py:258
  228.9 6.5 fusion.77
  238.4 7.5 %all_gather.35 = bf16[1024,128]{1,0:T(8,128)(2,1)S(1)} all-gather(bf16[256,128]{1,0:T(8,128)(2,1)S(1)} %fusion.100), channel_id=1, replica_groups=mesh['dp'=8,'tensor'=4] {'tensor'}, dimensions={0}, use_global_device_ids=true | all-gather | bytes 327680 | tf_op jit(solution)/shard_map/all_gather | solution.py:276
  245.9 6.5 all-gather.11.cloned.1.call-done
  252.4 2.4 fusion.154
  255.1 5.5 gather_fusion.1
  260.6 2.0 copy.68
  263.9 62.3 %while.33 = (s32[]{:T(128)}, bf16[2,512,4,64]{1,3,2,0:T(8,128)(2,1)}, bf16[2,512,4,64]{1,3,2,0:T(8,128)(2,1)}, bf16[2,512,4,64]{1,3,2,0:T(8,128)(2,1)}, bf16[102...) while((s32[]{:T(128)}, ...), condition=%wide.region_17.19_spmd, body=%wide.region_15.18_spmd.sunk | while | flops 686298624 | bytes 57437636 | solution.py:112
  269.4 2.8 fusion.230
  272.2 3.3 subtract_exponential_fusion.3
  275.5 7.9 %fusion.232 = bf16[2,512,4,64]{1,3,2,0:T(8,128)(2,1)} fusion(bf16[2,512,4,64]{1,3,2,0:T(8,128)(2,1)} %get-tuple-element.497, s32[]{:T(128)S(6)} %copy.112, f32[4,512,512]{1,2,0:T(8,128)} %subtract_exponential_fusion.3, f32[4,512,512]{1,2,0:T(8,128)} %fusion.230, bf16[1024,1,4,64]{0,3,2,1:T(8,128)(2,1)} %copy-done.5, s32[]{:T(128)S(6)} %select_n.203), kind=kOutput, calls=%fused_computation.43.clone.1 | convolution fusion | flops 139463168 | bytes 17563656 | tf_op jit(solution)/shard_map/while/body/eval_jaxpr/hqk,qhc->khc/dot_general | solution.py:102
  283.4 8.1 %fusion.231 = bf16[2,512,4,64]{1,3,2,0:T(8,128)(2,1)} fusion(bf16[2,512,4,64]{1,3,2,0:T(8,128)(2,1)} %get-tuple-element.496, s32[]{:T(128)S(6)} %copy.112, f32[4,512,512]{1,2,0:T(8,128)} %subtract_exponential_fusion.3, f32[4,512,512]{1,2,0:T(8,128)} %fusion.230, bf16[1024,1,4,64]{0,3,2,1:T(8,128)(2,1)} %copy-done.4, s32[]{:T(128)S(6)} %select_n.203), kind=kOutput, calls=%fused_computation.41.clone.1 | convolution fusion | flops 139463168 | bytes 17563656 | tf_op jit(solution)/shard_map/while/body/eval_jaxpr/hqk,khc->qhc/dot_general | solution.py:101
  291.5 3.7 fusion.233
  300.5 2.8 fusion.230
  303.4 3.3 subtract_exponential_fusion.3
  306.7 7.9 %fusion.232 = bf16[2,512,4,64]{1,3,2,0:T(8,128)(2,1)} fusion(bf16[2,512,4,64]{1,3,2,0:T(8,128)(2,1)} %get-tuple-element.497, s32[]{:T(128)S(6)} %copy.112, f32[4,512,512]{1,2,0:T(8,128)} %subtract_exponential_fusion.3, f32[4,512,512]{1,2,0:T(8,128)} %fusion.230, bf16[1024,1,4,64]{0,3,2,1:T(8,128)(2,1)} %copy-done.5, s32[]{:T(128)S(6)} %select_n.203), kind=kOutput, calls=%fused_computation.43.clone.1 | convolution fusion | flops 139463168 | bytes 17563656 | tf_op jit(solution)/shard_map/while/body/eval_jaxpr/hqk,qhc->khc/dot_general | solution.py:102
  314.6 8.0 %fusion.231 = bf16[2,512,4,64]{1,3,2,0:T(8,128)(2,1)} fusion(bf16[2,512,4,64]{1,3,2,0:T(8,128)(2,1)} %get-tuple-element.496, s32[]{:T(128)S(6)} %copy.112, f32[4,512,512]{1,2,0:T(8,128)} %subtract_exponential_fusion.3, f32[4,512,512]{1,2,0:T(8,128)} %fusion.230, bf16[1024,1,4,64]{0,3,2,1:T(8,128)(2,1)} %copy-done.4, s32[]{:T(128)S(6)} %select_n.203), kind=kOutput, calls=%fused_computation.41.clone.1 | convolution fusion | flops 139463168 | bytes 17563656 | tf_op jit(solution)/shard_map/while/body/eval_jaxpr/hqk,khc->qhc/dot_general | solution.py:101
  322.6 3.7 fusion.233
  326.2 2.4 copy.85
  328.6 3.9 reshape.388
  332.5 2.3 copy.83
  334.8 4.8 reshape.386
  341.1 4.8 reshape.387
  345.8 5.8 pad_maximum_fusion.2
  351.7 10.2 %gather_fusion.3 = bf16[1024,3,256]{2,1,0:T(4,128)(2,1)} fusion(bf16[1024,3,256]{2,1,0:T(4,128)(2,1)} %pad_maximum_fusion.2, s32[1024]{0:T(1024)S(1)} %copy-done.46), kind=kCustom, calls=%fused_computation.1.clone | custom fusion | bytes 3149824 | tf_op jit(solution)/shard_map/jit(_take)/gather | solution.py:290
  361.9 5.6 broadcast_select_fusion
  368.9 3.7 bitcast_convert_fusion
  372.7 2.0 fusion.122
  374.7 1.9 fusion.119
  376.6 2.1 fusion.132
  378.7 27.3 %reduce-scatter.11.cloned.1.call-done = bf16[256,1152]{1,0:T(8,128)(2,1)} async-done(((bf16[1024,1152]{1,0:T(8,128)(2,1)}), bf16[256,1152]{1,0:T(8,128)(2,1)}) %reduce-scatter.11.cloned.1.call-update) | async-done | bytes 589840 | tf_op jit(solution)/shard_map/reduce_scatter | solution.py:296
  409.4 2.8 convolution_convert_fusion.2
  412.2 4.8 convolution_convert_fusion.1
  419.4 42.3 %all-reduce.9.cloned.1.call-done = (f32[1024,128]{1,0:T(8,128)}, f32[128,1024]{1,0:T(8,128)}, f32[1024,128]{1,0:T(8,128)}, f32[128,1024]{1,0:T(8,128)}) async-done(((f32[1024,128]{1,0:T(8,128)}, f32[128,1024]{1,0:T(8,128)}, f32[1024,128]{1,0:T(8,128)}, f32[128,1024]{1,0:T(8,128)}), (f32[1024,128]{1,0:T(8,128)}, f32[128,1024]{1,0:T(8,128)}, f32[1024,128]{1,0:T(8,128)}, ...) | async-done | bytes 2097168 | tf_op jit(solution)/shard_map/psum | solution.py:310
  461.8 2.4 fusion.95
  464.2 77.9 %all-reduce.11.cloned.1.call-done = (bf16[128,3,256]{2,0,1:T(8,128)(2,1)}, bf16[256,128]{1,0:T(8,128)(2,1)}, bf16[128,1024]{1,0:T(8,128)(2,1)}, bf16[1024,128]{1,0:T(8,128)(2,1)}) async-done(((bf16[128,3,256]{2,0,1:T(8,128)(2,1)}, bf16[256,128]{1,0:T(8,128)(2,1)}, bf16[128,1024]{1,0:T(8,128)(2,1)}, bf16[1024,128]{1,0:T(8,128)(2,1)}), (bf16[128,3,256]{2,0,1:T(8,128)(2,1)}, bf16[256,128]{1,0:T(8,128)(2,1)}, ...) | async-done | bytes 786448 | tf_op jit(solution)/shard_map/psum | solution.py:316
  545.3 1.8 convert_element_type.148
  547.1 1.8 convert_element_type.150
  552.6 96.3 %all-reduce.7.cloned.1.call-done = (f32[1024,128]{1,0:T(8,128)}, f32[128,1024]{1,0:T(8,128)}, f32[1024,128]{1,0:T(8,128)}, f32[128,1024]{1,0:T(8,128)}) async-done(((f32[1024,128]{1,0:T(8,128)}, f32[128,1024]{1,0:T(8,128)}, f32[1024,128]{1,0:T(8,128)}, f32[128,1024]{1,0:T(8,128)}), (f32[1024,128]{1,0:T(8,128)}, f32[128,1024]{1,0:T(8,128)}, f32[1024,128]{1,0:T(8,128)}, ...) | async-done | bytes 2097168 | tf_op jit(solution)/shard_map/psum | solution.py:309
  648.8 1.9 copy.141
  650.7 1.9 copy.142
  652.6 1.9 copy.143
  654.4 1.9 copy.144
  (280 shorter events, 68.8 us)
Async XLA Ops:
  7.2 147.8 %copy-start = (bf16[1024,128]{1,0:T(8,128)(2,1)S(1)}, bf16[1024,128]{1,0:T(8,128)(2,1)}, u32[]{:S(2)}) copy-start(bf16[1024,128]{1,0:T(8,128)(2,1)} %param.52) | copy-start | bytes 786436
  7.2 31.6 %all-gather.5.cloned.1.call-start = ((), (), s32[]{:S(2)}) async-start(), calls=%async_computation.4 | async-start | bytes 2621440 | tf_op jit(solution)/shard_map/all_gather | solution.py:196
  8.5 9.3 %copy-start.44 = (f32[256]{0:T(256)}, f32[256]{0:T(256)S(1)}, u32[]{:S(2)}) copy-start(f32[256]{0:T(256)S(1)} %broadcast_multiply_fusion.1) | copy-start | bytes 3076
  9.8 9.0 %copy-start.61 = (f32[256]{0:T(256)}, f32[256]{0:T(256)S(1)}, u32[]{:S(2)}) copy-start(f32[256]{0:T(256)S(1)} %fusion.103) | copy-start | bytes 3076
  9.8 8.9 %copy-start.53 = (f32[256]{0:T(256)}, f32[256]{0:T(256)S(1)}, u32[]{:S(2)}) copy-start(f32[256]{0:T(256)S(1)} %fusion.138) | copy-start | bytes 3076
  12.0 111.5 %reduce-scatter.5.cloned.1.call-start = ((), (), s32[]{:S(2)}) async-start(), calls=%async_computation.5 | async-start | bytes 2949120 | tf_op jit(solution)/shard_map/reduce_scatter | solution.py:207
  12.8 4.3 copy-start.51
  17.2 14.6 %copy-start.65 = (s32[128]{0:T(128)}, s32[128]{0:T(128)S(1)}, u32[]{:S(2)}) copy-start(s32[128]{0:T(128)S(1)} %and_select_fusion) | copy-start | bytes 1540
  29.6 13.1 %copy-start.22 = (bf16[1024,128]{1,0:T(8,128)(2,1)}, bf16[1024,128]{1,0:T(8,128)(2,1)S(1)}, u32[]{:S(2)}) copy-start(bf16[1024,128]{1,0:T(8,128)(2,1)S(1)} %all_gather.29) | copy-start | bytes 786436
  31.7 21.5 %copy-start.56 = (pred[1024]{0:T(1024)(128)(4,1)}, pred[1024]{0:T(1024)(128)(4,1)S(1)}, u32[]{:S(2)}) copy-start(pred[1024]{0:T(1024)(128)(4,1)S(1)} %compare_and_fusion) | copy-start | bytes 3076
  32.4 10.2 %copy-start.40 = (bf16[128,3,256]{2,0,1:T(8,128)(2,1)S(1)}, bf16[128,3,256]{2,0,1:T(8,128)(2,1)}, u32[]{:S(2)}) copy-start(bf16[128,3,256]{2,0,1:T(8,128)(2,1)} %param.49) | copy-start | bytes 589828
  53.3 9.2 %copy-start.73 = (s32[1,2]{1,0:T(1,128)S(1)}, s32[1,2]{1,0:T(1,128)}, u32[]{:S(2)}) copy-start(s32[1,2]{1,0:T(1,128)} %param.33) | copy-start | bytes 28
  79.8 5.7 copy-start.34
  88.6 34.9 %copy-start.2 = (bf16[256,1024]{1,0:T(8,128)(2,1)S(1)}, bf16[256,1024]{1,0:T(8,128)(2,1)}, u32[]{:S(2)}) copy-start(bf16[256,1024]{1,0:T(8,128)(2,1)} %param.31) | copy-start | bytes 1572868
  90.3 58.1 %all-gather.9.cloned.1.call-start = ((), (), s32[]{:S(2)}) async-start(), calls=%async_computation.8 | async-start | bytes 2621440 | tf_op jit(solution)/shard_map/all_gather | solution.py:239
  91.2 81.8 %all-gather.7.cloned.1.call-start = ((), (), s32[]{:S(2)}) async-start(), calls=%async_computation.6 | async-start | bytes 2621440 | tf_op jit(solution)/shard_map/all_gather | solution.py:218
  128.2 95.3 %reduce-scatter.9.cloned.1.call-start = ((), (), s32[]{:S(2)}) async-start(), calls=%async_computation.9 | async-start | bytes 2949120 | tf_op jit(solution)/shard_map/reduce_scatter | solution.py:258
  136.1 18.8 %copy-start.15 = (bf16[256,1024]{1,0:T(8,128)(2,1)S(1)}, bf16[256,1024]{1,0:T(8,128)(2,1)}, u32[]{:S(2)}) copy-start(bf16[256,1024]{1,0:T(8,128)(2,1)} %add_convert_fusion.1) | copy-start | bytes 1572868
  161.0 16.6 %copy-start.20 = (bf16[1024,128]{1,0:T(8,128)(2,1)}, bf16[1024,128]{1,0:T(8,128)(2,1)S(1)}, u32[]{:S(2)}) copy-start(bf16[1024,128]{1,0:T(8,128)(2,1)S(1)} %all_gather.31) | copy-start | bytes 786436
  161.0 16.6 %copy-start.36 = (bf16[128,1024]{1,0:T(8,128)(2,1)S(1)}, bf16[128,1024]{1,0:T(8,128)(2,1)}, u32[]{:S(2)}) copy-start(bf16[128,1024]{1,0:T(8,128)(2,1)} %param.53) | copy-start | bytes 786436
  173.0 4.6 copy-start.67
  181.5 4.6 copy-start.69
  186.1 38.7 %copy-start.48 = (f32[256]{0:T(256)S(1)}, f32[256]{0:T(256)}, u32[]{:S(2)}) copy-start(f32[256]{0:T(256)} %copy-done.47) | copy-start | bytes 3076
  186.1 38.7 %copy-start.49 = (f32[1024]{0:T(1024)S(1)}, f32[1024]{0:T(1024)}, u32[]{:S(2)}) copy-start(f32[1024]{0:T(1024)} %param.42) | copy-start | bytes 12292
  190.3 35.0 %copy-start.64 = (f32[256]{0:T(256)S(1)}, f32[256]{0:T(256)}, u32[]{:S(2)}) copy-start(f32[256]{0:T(256)} %copy-done.63) | copy-start | bytes 3076
  190.3 35.5 %copy-start.60 = (f32[256]{0:T(256)S(1)}, f32[256]{0:T(256)}, u32[]{:S(2)}) copy-start(f32[256]{0:T(256)} %copy-done.59) | copy-start | bytes 3076
  190.3 62.0 %all-gather.11.cloned.1.call-start = ((), (), s32[]{:S(2)}) async-start(), calls=%async_computation.10 | async-start | bytes 2621440 | tf_op jit(solution)/shard_map/all_gather | solution.py:275
  224.8 4.1 copy-start.72
  226.2 9.2 %copy-start.57 = (f32[256]{0:T(256)}, f32[256]{0:T(256)S(1)}, u32[]{:S(2)}) copy-start(f32[256]{0:T(256)S(1)} %negate_multiply_fusion.1) | copy-start | bytes 3076
  228.2 146.5 %reduce-scatter.7.cloned.1.call-start = ((), (), s32[]{:S(2)}) async-start(), calls=%async_computation.7 | async-start | bytes 2949120 | tf_op jit(solution)/shard_map/reduce_scatter | solution.py:227
  238.0 168.0 %reduce-scatter.11.cloned.1.call-start = ((), (), s32[]{:S(2)}) async-start(), calls=%async_computation.11 | async-start | bytes 2949120 | tf_op jit(solution)/shard_map/reduce_scatter | solution.py:296
  245.9 14.8 %copy-start.32 = (bf16[1024,128]{1,0:T(8,128)(2,1)}, bf16[1024,128]{1,0:T(8,128)(2,1)S(1)}, u32[]{:S(2)}) copy-start(bf16[1024,128]{1,0:T(8,128)(2,1)S(1)} %all_gather.35) | copy-start | bytes 786436
  263.9 5.1 copy-start.74
  283.4 11.7 %copy-start.75 = (s32[2]{0:T(128)S(1)}, s32[2]{0:T(128)}, u32[]{:S(2)}) copy-start(s32[2]{0:T(128)} %copy-done.74) | copy-start | bytes 28 | tf_op jit(solution)/shard_map/while
  295.1 5.1 copy-start.74
  314.6 11.7 %copy-start.75 = (s32[2]{0:T(128)S(1)}, s32[2]{0:T(128)}, u32[]{:S(2)}) copy-start(s32[2]{0:T(128)} %copy-done.74) | copy-start | bytes 28 | tf_op jit(solution)/shard_map/while
  326.2 13.4 %copy-start.35 = (bf16[2,512,4,64]{1,3,2,0:T(8,128)(2,1)S(1)}, bf16[2,512,4,64]{1,3,2,0:T(8,128)(2,1)}, u32[]{:S(2)}) copy-start(bf16[2,512,4,64]{1,3,2,0:T(8,128)(2,1)} %get-tuple-element.261) | copy-start | bytes 1572868
  339.6 12.0 %copy-start.46 = (s32[1024]{0:T(1024)S(1)}, s32[1024]{0:T(1024)}, u32[]{:S(2)}) copy-start(s32[1024]{0:T(1024)} %get-tuple-element.330) | copy-start | bytes 12292
  345.8 16.0 %copy-start.55 = (pred[1024]{0:T(1024)(128)(4,1)S(1)}, pred[1024]{0:T(1024)(128)(4,1)}, u32[]{:S(2)}) copy-start(pred[1024]{0:T(1024)(128)(4,1)} %compare_and_fusion.1) | copy-start | bytes 3076
  351.7 17.2 %copy-start.41 = (bf16[128,3,256]{2,0,1:T(8,128)(2,1)S(1)}, bf16[128,3,256]{2,0,1:T(8,128)(2,1)}, u32[]{:S(2)}) copy-start(bf16[128,3,256]{2,0,1:T(8,128)(2,1)} %param.49) | copy-start | bytes 589828
  361.9 7.0 %copy-start.70 = (bf16[1024,3,256]{2,0,1:T(8,128)(2,1)S(1)}, bf16[1024,3,256]{2,0,1:T(8,128)(2,1)}, u32[]{:S(2)}) copy-start(bf16[1024,3,256]{2,0,1:T(8,128)(2,1)} %param.38) | copy-start | bytes 4718596
  368.9 5.8 copy-start.11
  372.6 35.6 %copy-start.14 = (bf16[256,1024]{1,0:T(8,128)(2,1)S(1)}, bf16[256,1024]{1,0:T(8,128)(2,1)}, u32[]{:S(2)}) copy-start(bf16[256,1024]{1,0:T(8,128)(2,1)} %fusion.106) | copy-start | bytes 1572868
  372.6 36.8 %copy-start.21 = (bf16[1024,128]{1,0:T(8,128)(2,1)S(1)}, bf16[1024,128]{1,0:T(8,128)(2,1)}, u32[]{:S(2)}) copy-start(bf16[1024,128]{1,0:T(8,128)(2,1)} %copy-done.20) | copy-start | bytes 786436
  372.6 89.1 %all-reduce.9.cloned.1.call-start = ((), (), s32[]{:S(2)}) async-start(), calls=%async_computation.13 | async-start | bytes 4194304 | tf_op jit(solution)/shard_map/psum | solution.py:310
  376.6 35.6 %copy-start.38 = (bf16[1024,128]{1,0:T(8,128)(2,1)S(1)}, bf16[1024,128]{1,0:T(8,128)(2,1)}, u32[]{:S(2)}) copy-start(bf16[1024,128]{1,0:T(8,128)(2,1)} %all_gather.33) | copy-start | bytes 786436
  409.4 132.8 %all-reduce.11.cloned.1.call-start = ((), (), s32[]{:S(2)}) async-start(), calls=%async_computation.14 | async-start | bytes 1572864 | tf_op jit(solution)/shard_map/psum | solution.py:316
  412.2 4.9 copy-start.26
  412.2 4.9 copy-start.33
  412.2 6.0 copy-start.18
  412.2 6.0 copy-start.23
  417.0 44.7 %copy-start.30 = (bf16[128,1024]{1,0:T(8,128)(2,1)S(1)}, bf16[128,1024]{1,0:T(8,128)(2,1)}, u32[]{:S(2)}) copy-start(bf16[128,1024]{1,0:T(8,128)(2,1)} %param.55) | copy-start | bytes 786436
  417.0 44.7 %copy-start.68 = (f32[1024]{0:T(1024)S(1)}, f32[1024]{0:T(1024)}, u32[]{:S(2)}) copy-start(f32[1024]{0:T(1024)} %param.47) | copy-start | bytes 12292
  419.3 129.6 %copy-start.3 = (bf16[256,1024]{1,0:T(8,128)(2,1)S(1)}, bf16[256,1024]{1,0:T(8,128)(2,1)}, u32[]{:S(2)}) copy-start(bf16[256,1024]{1,0:T(8,128)(2,1)} %param.31) | copy-start | bytes 1572868
  419.3 129.6 %copy-start.31 = (bf16[1024,128]{1,0:T(8,128)(2,1)S(1)}, bf16[1024,128]{1,0:T(8,128)(2,1)}, u32[]{:S(2)}) copy-start(bf16[1024,128]{1,0:T(8,128)(2,1)} %param.48) | copy-start | bytes 786436
  419.3 129.6 %copy-start.45 = (f32[256]{0:T(256)S(1)}, f32[256]{0:T(256)}, u32[]{:S(2)}) copy-start(f32[256]{0:T(256)} %copy-done.44) | copy-start | bytes 3076
  419.3 129.6 %copy-start.50 = (f32[1024]{0:T(1024)S(1)}, f32[1024]{0:T(1024)}, u32[]{:S(2)}) copy-start(f32[1024]{0:T(1024)} %param.36) | copy-start | bytes 12292
  419.4 229.5 %all-reduce.7.cloned.1.call-start = ((), (), s32[]{:S(2)}) async-start(), calls=%async_computation.12 | async-start | bytes 4194304 | tf_op jit(solution)/shard_map/psum | solution.py:309
  461.7 89.0 %copy-start.62 = (f32[256]{0:T(256)S(1)}, f32[256]{0:T(256)}, u32[]{:S(2)}) copy-start(f32[256]{0:T(256)} %copy-done.61) | copy-start | bytes 3076
  461.7 89.0 %copy-start.54 = (f32[256]{0:T(256)S(1)}, f32[256]{0:T(256)}, u32[]{:S(2)}) copy-start(f32[256]{0:T(256)} %copy-done.53) | copy-start | bytes 3076
  461.7 89.4 %copy-start.8 = (f32[256,1024]{1,0:T(8,128)S(1)}, f32[256,1024]{1,0:T(8,128)}, u32[]{:S(2)}) copy-start(f32[256,1024]{1,0:T(8,128)} %param.32) | copy-start | bytes 3145732
  461.8 89.4 %copy-start.58 = (f32[256]{0:T(256)S(1)}, f32[256]{0:T(256)}, u32[]{:S(2)}) copy-start(f32[256]{0:T(256)} %copy-done.57) | copy-start | bytes 3076
  464.2 87.0 %copy-start.10 = (f32[256,1024]{1,0:T(8,128)S(1)}, f32[256,1024]{1,0:T(8,128)}, u32[]{:S(2)}) copy-start(f32[256,1024]{1,0:T(8,128)} %copy-done.9) | copy-start | bytes 3145732
  551.1 105.2 %copy-start.1 = (bf16[1024,128]{1,0:T(8,128)(2,1)S(1)}, bf16[1024,128]{1,0:T(8,128)(2,1)}, u32[]{:S(2)}) copy-start(bf16[1024,128]{1,0:T(8,128)(2,1)} %param.52) | copy-start | bytes 786436
  (28 other events, 58.6 us)
Sparse Core Ops, SparseCore 0:
  12.1 26.6 all-gather.4
  90.4 33.0 reduce-scatter.4
  125.7 22.5 all-gather.8
  150.4 22.5 all-gather.6
  190.4 33.0 reduce-scatter.8
  228.3 23.9 all-gather.10
  254.9 33.0 reduce-scatter.6
  372.8 33.2 reduce-scatter.10
  409.7 51.9 all-reduce.8
  466.9 75.2 all-reduce.10
  546.1 102.6 all-reduce.6
